TPU v7x, 32 devices: a whole 2x2x4 slice. The times are simulated.
32 devices in a mesh: ctx: 4 (over y, x), tp: 4 (over z), grp: 2 (over core).
Axes of the slice: x: 2, y: 2, z: 4, core: 2. Of those that a mesh axis runs over, the one named last changes fastest.
Arguments:
- patches: bfloat16 [32, 5120], P('ctx'), may hold values from -6 to 6
- route_count: int32 [4, 4], replicated, may hold values from 0 to 2, as said below
- text_states: bfloat16 [512, 4096], P('ctx', ('tp', 'grp')), may hold values from -6 to 6
- segment_ids: int32 [512], replicated, may hold values from 0 to 3, never falling along the last dimension, each value on 1 to 256 neighbouring positions
- vision_gain: float32 [1280], replicated, may hold values from 0.1 to 1.9
- merge_up: bfloat16 [5120, 2560], P(None, ('tp', 'grp')), may hold values from -0.078125 to 0.078125
- merge_down: bfloat16 [2560, 4096], P(('tp', 'grp')), may hold values from -0.125 to 0.125
- norm_gain: float32 [4096], replicated, may hold values from 0.1 to 1.9
- query_weight: bfloat16 [4096, 4096], P(None, ('tp', 'grp')), may hold values from -0.62928387 to 0.62928387
- kv_weight: bfloat16 [4096, 2048], P(None, 'tp'), may hold values from -0.4578688 to 0.4578688
Outputs:
- attended: bfloat16 [512, 4096], P('ctx', ('tp', 'grp'))
Inputs may be any that keep to these rules, and one draw needn't show every extreme that they name: route_count[c, d] counts the live rows among the 2 rows that source c holds for owner d; at least one owner gets 2 live rows from every source. `segment_ids`: never falling along the packed batch; a segment has at most 256 positions.
All inputs are finite; a program needn't handle non-finite values.
Results may differ from a plain program's by a relative error of at most 0.04.
Values may be sent and summed in bfloat16 or wider, within the bound.
A program may use at most 64 MiB of HBM per device.

v0:
```python
import jax
import jax.numpy as jnp
from jax import lax
from jax.sharding import PartitionSpec as P

HQ = 32
KVH = 8
HD = 128
EPSILON = 1e-06
NEGATIVE = -1e30


def rms_scale(values, gain):
    mean_square = jnp.mean(values * values, axis=-1, keepdims=True)
    return values * lax.rsqrt(mean_square + EPSILON) * gain


def attend(
    running,
    queries4,
    shard_piece,
    key_pos,
    query_pos,
    query_seg,
    segment_ids,
    visual_count,
    tokens_dev,
):
    weighted, running_max, denominator = running
    piece_rows = shard_piece.shape[0]
    kv_heads = queries4.shape[1]
    kv_split = shard_piece.reshape(piece_rows, kv_heads, 2, HD)
    key_block = kv_split[:, :, 0]
    value_block = kv_split[:, :, 1]
    key_owner = key_pos // tokens_dev
    owner_match = key_owner[:, None] == jnp.arange(visual_count.shape[0], dtype=jnp.int32)[None, :]
    visual_limit = jnp.sum(jnp.where(owner_match, visual_count[None, :], 0), axis=1)
    key_visual = key_pos % tokens_dev < visual_limit
    key_seg = segment_ids[key_pos]
    allowed = (query_seg[:, None] == key_seg[None, :]) & (
        key_visual[None, :] | (key_pos[None, :] <= query_pos[:, None])
    )
    scores = jnp.where(
        allowed,
        jnp.einsum("qkgd,rkd->kgqr", queries4, key_block, preferred_element_type=jnp.float32)
        * HD ** (-0.5),
        NEGATIVE,
    )
    new_max = jnp.maximum(running_max, jnp.max(scores, axis=-1))
    weights = jnp.exp(jnp.where(allowed, scores - new_max[..., None], NEGATIVE))
    denominator = jnp.sum(weights, axis=-1)
    weighted = jnp.einsum(
        "kgqr,rkd->kgqd",
        weights.astype(jnp.bfloat16),
        value_block,
        preferred_element_type=jnp.float32,
    )
    return (weighted, new_max, denominator)


def start_state(kv_heads, per_head, tokens_dev):
    return (
        jnp.zeros((kv_heads, per_head, tokens_dev, HD), jnp.float32),
        jnp.full((kv_heads, per_head, tokens_dev), NEGATIVE, jnp.float32),
        jnp.zeros((kv_heads, per_head, tokens_dev), jnp.float32),
    )


def shards(
    patches,
    route_count,
    text_states,
    segment_ids,
    vision_gain,
    merge_up,
    merge_down,
    norm_gain,
    query_weight,
    kv_weight,
):
    ctx_size = lax.axis_size("ctx")
    grp_size = lax.axis_size("grp")
    tp_size = lax.axis_size("tp")
    owner_index = lax.axis_index("ctx")
    member = lax.axis_index("grp")
    tp_index = lax.axis_index("tp")
    tensor_index = tp_index * grp_size + member
    row_count = patches.shape[0]
    bucket_rows = row_count // ctx_size
    tokens_dev = text_states.shape[0]
    grouped = patches.astype(jnp.float32).reshape(row_count, 4, -1)
    patch_normed = rms_scale(grouped, vision_gain).reshape(row_count, -1).astype(jnp.bfloat16)
    hidden = jax.nn.gelu(
        jnp.dot(patch_normed, merge_up, preferred_element_type=jnp.float32), approximate=False
    ).astype(jnp.bfloat16)
    partial_value = jnp.dot(hidden, merge_down, preferred_element_type=jnp.float32)
    column = lax.dynamic_slice_in_dim(route_count, owner_index, 1, 1)[:, 0]
    count_ends = jnp.cumsum(column)
    count_starts = count_ends - column
    slot_ids = jnp.arange(tokens_dev, dtype=jnp.int32)
    source = jnp.sum((count_ends[None, :] <= slot_ids[:, None]).astype(jnp.int32), axis=1)
    source = jnp.minimum(source, ctx_size - 1)
    source_match = source[:, None] == jnp.arange(ctx_size, dtype=jnp.int32)[None, :]
    first_slot = jnp.sum(jnp.where(source_match, count_starts[None, :], 0), axis=1)
    visual = slot_ids < count_ends[ctx_size - 1]
    pick_rows = jnp.where(visual, source * bucket_rows + slot_ids - first_slot, 0)
    merged = lax.psum(partial_value, ("tp", "grp")).astype(jnp.bfloat16)
    arrived = lax.all_to_all(
        merged.reshape(ctx_size, bucket_rows, -1), "ctx", split_axis=0, concat_axis=0, tiled=True
    )
    arrived = arrived.reshape(row_count, -1)
    text_full = lax.all_gather(text_states, ("tp", "grp"), axis=1, tiled=True)
    packed = jnp.where(visual[:, None], arrived[pick_rows], text_full)
    normal = rms_scale(packed.astype(jnp.float32), norm_gain).astype(jnp.bfloat16)
    queries = jnp.dot(normal, query_weight, preferred_element_type=jnp.float32).astype(jnp.bfloat16)
    kv_pairs = jnp.dot(normal, kv_weight, preferred_element_type=jnp.float32).astype(jnp.bfloat16)
    heads_dev = queries.shape[1] // HD
    group = HQ // KVH
    kv_per_tp = KVH // tp_size
    query_pos = owner_index * tokens_dev + slot_ids
    query_seg = segment_ids[query_pos]
    visual_count = jnp.sum(route_count, axis=0)
    kv_local = tensor_index * heads_dev // group - tp_index * kv_per_tp
    chosen = lax.dynamic_slice_in_dim(kv_pairs, kv_local * 2 * HD, 2 * HD, 1)
    queries4 = queries.reshape(tokens_dev, 1, heads_dev, HD)
    shard_piece = lax.all_gather(chosen, "ctx", axis=0, tiled=True)
    key_pos = jnp.arange(shard_piece.shape[0], dtype=jnp.int32)
    weighted, running_max, denominator = attend(
        start_state(1, heads_dev, tokens_dev),
        queries4,
        shard_piece,
        key_pos,
        query_pos,
        query_seg,
        segment_ids,
        visual_count,
        tokens_dev,
    )
    result = (weighted / denominator[..., None]).reshape(heads_dev, tokens_dev, HD)
    return result.transpose(1, 0, 2).reshape(tokens_dev, -1).astype(jnp.bfloat16)


def solution(mesh):
    return jax.shard_map(
        shards,
        mesh=mesh,
        in_specs=(
            P("ctx", None),
            P(),
            P("ctx", ("tp", "grp")),
            P(),
            P(),
            P(None, ("tp", "grp")),
            P(("tp", "grp"), None),
            P(),
            P(None, ("tp", "grp")),
            P(None, "tp"),
        ),
        out_specs=P("ctx", ("tp", "grp")),
        check_vma=False,
    )
```

profile of v0, /device:TPU:0, one launch (start us, length us, event | category | flops | bytes accessed | tf_op | source)
XLA Modules:
  0.0 106.3 jit_solution(12033060647353405200)
XLA Ops:
  6.5 1.0 convert_multiply_fusion.3
  7.6 0.1 reduce_sum.67
  7.7 0.7 mul.112
  8.5 4.6 %fusion.41 = f32[8,4096]{1,0:T(8,128)} fusion(bf16[320,4096]{1,0:T(8,128)(2,1)} %param.16, bf16[5120,320]{0,1:T(8,128)(2,1)S(1)} %copy-done, f32[8,5120]{1,0:T(8,128)S(1)} %bitcast.59, bf16[8,5120]{1,0:T(8,128)(2,1)} %param.10, f32[5120]{0:T(1024)S(1)} %mul.113), kind=kOutput, calls=%fused_computation.58 | convolution fusion | flops 47516160 | bytes 6295552 | tf_op jit(solution)/shard_map/dot_general | solution.py:96
  13.1 32.0 %all-reduce.1 = bf16[8,4096]{1,0:T(8,128)(2,1)S(1)} all-reduce(f32[8,4096]{1,0:T(8,128)} %fusion.41), channel_id=1, replica_groups=mesh['ctx'=4,'tp'=4,'grp'=2] {'tp','grp'}, use_global_device_ids=true, to_apply=%region_4.5 | all-reduce | flops 32768 | bytes 196608 | tf_op jit(solution)/shard_map/psum | solution.py:107
  45.2 0.7 reshape.183
  45.8 3.7 %all-to-all-start = ((bf16[4,2,4096]{2,1,0:T(2,128)(2,1)}), bf16[4,2,4096]{2,1,0:T(2,128)(2,1)S(1)}, u32[]{:S(2)}, u32[]{:S(2)}) async-start(bf16[4,2,4096]{2,1,0:T(2,128)(2,1)} %reshape.183), calls=%async_computation | async-start | bytes 131072 | tf_op jit(solution)/shard_map/all_to_all | solution.py:108
  49.6 0.7 all-gather.2.cloned.1.call-update
  50.3 0.2 fusion.112
  50.6 0.1 reduce.2
  50.7 0.6 slice.10
  51.3 1.3 %gather_fusion = s32[128]{0:T(128)S(1)} fusion(s32[512]{0:T(512)S(1)} %copy-done.1, s32[1024]{0:T(1024)S(1)} %pad_clamp_fusion.1), kind=kCustom, calls=%fused_computation | custom fusion | bytes 1536 | tf_op jit(solution)/shard_map/gather | solution.py:121
  52.6 3.5 %gather_fusion.1 = s32[512]{0:T(512)S(1)} fusion(s32[512]{0:T(512)S(1)} %copy-done.1, s32[1024]{0:T(1024)S(1)} %pad_clamp_fusion), kind=kCustom, calls=%fused_computation.1 | custom fusion | bytes 6144 | tf_op jit(solution)/shard_map/gather | solution.py:39
  56.1 0.1 convert_reduce_fusion
  56.2 0.1 select_reduce_fusion.1
  56.3 0.7 fusion.80
  57.0 0.1 select_reduce_fusion
  57.1 0.8 fusion.19
  57.9 0.7 iota_compare_fusion.4
  58.7 2.2 %gather_fusion.2 = bf16[128,4096]{1,0:T(8,128)(2,1)} fusion(bf16[8,4096]{1,0:T(8,128)(2,1)S(1)} %reshape.184, s32[1024]{0:T(1024)S(1)} %pad_clamp_fusion.2), kind=kCustom, calls=%fused_computation.2 | custom fusion | bytes 2097664 | tf_op jit(solution)/shard_map/gather | solution.py:113
  60.9 12.1 %all-gather.2.cloned.1.call-done = bf16[128,4096]{1,0:T(8,128)(2,1)} async-done(((bf16[128,512]{1,0:T(8,128)(2,1)}), bf16[128,4096]{1,0:T(8,128)(2,1)}) %all-gather.2.cloned.1.call-update) | async-done | bytes 1048592 | tf_op jit(solution)/shard_map/all_gather | solution.py:112
  73.0 2.2 %fusion = (f32[128]{0:T(128)S(1)}, bf16[128,4096]{1,0:T(8,128)(2,1)S(1)}) fusion(bf16[128,4096]{1,0:T(8,128)(2,1)} %gather_fusion.2, bf16[128,4096]{1,0:T(8,128)(2,1)} %all-gather.2.cloned.1.call-done, pred[128]{0:T(512)(128)(4,1)S(1)} %iota_compare_fusion.4), kind=kLoop, calls=%fused_computation.5 | loop fusion | flops 2097024 | bytes 3146368 | tf_op jit(solution)/shard_map/reduce_sum | solution.py:14
  75.2 3.3 %fusion.16 = bf16[128,512]{1,0:T(8,128)(2,1)S(1)} fusion(bf16[4096,512]{1,0:T(8,128)(2,1)} %param.19, bf16[128,4096]{1,0:T(8,128)(2,1)S(1)} %get-tuple-element.6, f32[4096]{0:T(1024)S(1)} %copy-done.6, f32[128]{0:T(128)S(1)} %add_rsqrt_fusion.1), kind=kOutput, calls=%fused_computation.24 | convolution fusion | flops 538968064 | bytes 5390848 | tf_op jit(solution)/shard_map/dot_general | solution.py:116
  78.6 9.6 %all_gather.7 = bf16[512,256]{1,0:T(8,128)(2,1)} all-gather(bf16[128,256]{1,0:T(8,128)(2,1)S(1)} %dynamic-slice_convert_fusion), channel_id=1, replica_groups=mesh['ctx'=4,'tp'=4,'grp'=2] {'ctx'}, dimensions={0}, use_global_device_ids=true | all-gather | bytes 327680 | tf_op jit(solution)/shard_map/all_gather | solution.py:126
  88.2 1.0 reshape.185
  89.2 1.1 %fusion.113 = (bf16[512,1,1,128]{3,2,0,1:T(2,128)(2,1)}, bf16[512,1,1,128]{3,2,0,1:T(2,128)(2,1)S(1)}) fusion(bf16[512,1,2,128]{3,2,0,1:T(2,128)(2,1)S(1)} %reshape.185), kind=kLoop, calls=%fused_computation.155 | loop fusion | bytes 524288 | tf_op jit(solution)/shard_map/slice | solution.py:34
  90.3 3.3 %fusion.7 = bf16[16,4,8,128]{3,2,1,0:T(8,128)(2,1)S(1)} fusion(bf16[4096,512]{1,0:T(8,128)(2,1)} %param.18, bf16[128,4096]{1,0:T(8,128)(2,1)} %copy-done.2, f32[4096]{0:T(1024)S(1)} %copy-done.6, f32[128]{0:T(128)} %copy-done.7), kind=kOutput, calls=%fused_computation.15 | convolution fusion | flops 539033600 | bytes 5390848 | tf_op jit(solution)/shard_map/dot_general | solution.py:115
  93.6 1.3 %fusion.114 = (f32[4,128]{1,0:T(4,128)S(1)}, f32[1,4,128,512]{2,3,1,0:T(8,128)}) fusion(bf16[16,4,8,128]{3,2,1,0:T(8,128)(2,1)S(1)} %fusion.7, bf16[512,1,1,128]{3,2,0,1:T(2,128)(2,1)S(1)} %get-tuple-element.10, pred[128,512]{0,1:T(8,128)(4,1)S(1)} %copy-done.4), kind=kOutput, calls=%fused_computation.156 | convolution fusion | flops 67894784 | bytes 1378304 | tf_op jit(solution)/shard_map/qkgd,rkd->kgqr/dot_general | solution.py:45
  94.9 0.8 copy.27
  95.7 1.4 %fusion.8 = f32[4,128]{1,0:T(4,128)S(1)} fusion(f32[1,4,128,512]{2,3,1,0:T(8,128)} %get-tuple-element.12, f32[4,128]{1,0:T(4,128)S(1)} %broadcast_maximum_fusion, pred[128,512]{0,1:T(8,128)(4,1)} %fusion.19), kind=kLoop, calls=%fused_computation.18 | loop fusion | flops 785920 | bytes 1118208 | tf_op jit(solution)/shard_map/reduce_sum | solution.py:51
  97.1 1.6 %fusion.6 = bf16[128,4,128]{0,2,1:T(8,128)(2,1)S(1)} fusion(f32[1,4,128,512]{2,3,1,0:T(8,128)} %get-tuple-element.12, f32[4,128]{1,0:T(4,128)S(1)} %broadcast_maximum_fusion, pred[128,512]{0,1:T(8,128)(4,1)} %fusion.19, bf16[512,1,1,128]{0,3,2,1:T(8,128)(2,1)} %copy.27, f32[128,4]{0,1:T(4,128)S(1)} %bitcast.62), kind=kOutput, calls=%fused_computation.13 | convolution fusion | flops 68026368 | bytes 1380352 | tf_op jit(solution)/shard_map/kgqr,rkd->kgqd/dot_general | solution.py:52
  98.7 0.8 copy.25
  (37 shorter events, 0.3 us)
Async XLA Ops:
  6.5 2.0 %copy-start = (bf16[5120,320]{0,1:T(8,128)(2,1)S(1)}, bf16[5120,320]{0,1:T(8,128)(2,1)}, u32[]{:S(2)}) copy-start(bf16[5120,320]{0,1:T(8,128)(2,1)} %param.15) | copy-start | bytes 9830404
  8.5 41.8 %copy-start.5 = (s32[4,4]{1,0:T(4,128)S(1)}, s32[4,4]{1,0:T(4,128)}, u32[]{:S(2)}) copy-start(s32[4,4]{1,0:T(4,128)} %param.11) | copy-start | bytes 196
  8.5 42.8 %copy-start.1 = (s32[512]{0:T(512)S(1)}, s32[512]{0:T(512)}, u32[]{:S(2)}) copy-start(s32[512]{0:T(512)} %param.13) | copy-start | bytes 6148
  45.8 12.8 %all-to-all-start = ((bf16[4,2,4096]{2,1,0:T(2,128)(2,1)}), bf16[4,2,4096]{2,1,0:T(2,128)(2,1)S(1)}, u32[]{:S(2)}, u32[]{:S(2)}) async-start(bf16[4,2,4096]{2,1,0:T(2,128)(2,1)} %reshape.183), calls=%async_computation | async-start | bytes 131072 | tf_op jit(solution)/shard_map/all_to_all | solution.py:108
  49.6 23.5 %all-gather.2.cloned.1.call-start = ((), (), s32[]{:S(2)}) async-start(), calls=%async_computation.1 | async-start | bytes 1179648 | tf_op jit(solution)/shard_map/all_gather | solution.py:112
  60.9 14.3 %copy-start.6 = (f32[4096]{0:T(1024)S(1)}, f32[4096]{0:T(1024)}, u32[]{:S(2)}) copy-start(f32[4096]{0:T(1024)} %param.17) | copy-start | bytes 49156
  75.2 3.4 %copy-start.2 = (bf16[128,4096]{1,0:T(8,128)(2,1)}, bf16[128,4096]{1,0:T(8,128)(2,1)S(1)}, u32[]{:S(2)}) copy-start(bf16[128,4096]{1,0:T(8,128)(2,1)S(1)} %get-tuple-element.6) | copy-start | bytes 3145732
  75.2 3.4 %copy-start.7 = (f32[128]{0:T(128)}, f32[128]{0:T(128)S(1)}, u32[]{:S(2)}) copy-start(f32[128]{0:T(128)S(1)} %add_rsqrt_fusion.1) | copy-start | bytes 1540
  90.3 3.3 %copy-start.4 = (pred[128,512]{0,1:T(8,128)(4,1)S(1)}, pred[128,512]{0,1:T(8,128)(4,1)}, u32[]{:S(2)}) copy-start(pred[128,512]{0,1:T(8,128)(4,1)} %fusion.19) | copy-start | bytes 196612
  90.3 4.6 %copy-start.3 = (bf16[512,1,1,128]{3,2,0,1:T(2,128)(2,1)S(1)}, bf16[512,1,1,128]{3,2,0,1:T(2,128)(2,1)}, u32[]{:S(2)}) copy-start(bf16[512,1,1,128]{3,2,0,1:T(2,128)(2,1)} %get-tuple-element.9) | copy-start | bytes 393220
Sparse Core Ops, SparseCore 0:
  52.0 21.0 all-gather.1
where the time goes:
time: 107 us; the launch traced here: 106 us
  blocking collectives  41.6 us (39%)
  matrix products  14.1 us (13%)
  between operations  13.7 us (13%)
  local copies, waits for them, and re-layouts  13 us (12%)
  waiting for transfers between devices  12.8 us (12%)
  other arithmetic  7.46 us (7%)
  starting transfers between devices  3.72 us (3%)
    psum x1, blocking collectives, shards(): merged = lax.psum(partial_value, ('tp', 'grp')).astype(jnp.bfloat16)  32 us
    all_gather x1, waiting for transfers between devices, shards(): text_full = lax.all_gather(text_states, ('tp', 'grp'), axis=1, tiled=True)  12.1 us
    all_gather x1, blocking collectives, shards(): shard_piece = lax.all_gather(chosen, 'ctx', axis=0, tiled=True)  9.55 us
    dot_general x1, matrix products, shards(): jnp.dot(hidden, merge_down, preferred_element_type=jnp.float32)  4.57 us
    all_to_all x1, starting transfers between devices, shards(): lax.all_to_all(merged.reshape(ctx_size, bucket_rows, -1), 'ctx', split_ax...  3.72 us
    gather x1, local copies, waits for them, and re-layouts, attend(): key_seg = segment_ids[key_pos]  3.49 us
    dot_general x1, matrix products, shards(): jnp.dot(normal, kv_weight, preferred_element_type=jnp.float32)  3.34 us
    dot_general x1, matrix products, shards(): jnp.dot(normal, query_weight, preferred_element_type=jnp.float32)  3.32 us
  transfers between devices with their start and end apart: 2, of which 1 were waited for; matrix products, arithmetic and copies ran while one was open for 10% of the time, Pallas kernels for 0%

commit v1 on v0

--- a/solution.py
+++ b/solution.py
@@ -2,6 +2,7 @@
 import jax.numpy as jnp
 from jax import lax
 from jax.sharding import PartitionSpec as P
+from jax.lax import all_gather
 
 HQ = 32
 KVH = 8
@@ -104,7 +105,7 @@
     first_slot = jnp.sum(jnp.where(source_match, count_starts[None, :], 0), axis=1)
     visual = slot_ids < count_ends[ctx_size - 1]
     pick_rows = jnp.where(visual, source * bucket_rows + slot_ids - first_slot, 0)
-    merged = lax.psum(partial_value, ("tp", "grp")).astype(jnp.bfloat16)
+    merged = jnp.sum(all_gather(partial_value, ("tp", "grp")), axis=0).astype(jnp.bfloat16)
     arrived = lax.all_to_all(
         merged.reshape(ctx_size, bucket_rows, -1), "ctx", split_axis=0, concat_axis=0, tiled=True
     )

time: 107 us -> 95.6 us (0.89)
  blocking collectives: 41.6 us -> 9.63 us
  waiting for transfers between devices: 12.8 us -> 32.5 us
  other arithmetic: 7.46 us -> 8.6 us
    psum x1 -> x0, blocking collectives: 32 us -> none  [shards(): merged = lax.psum(partial_value, ('tp', 'grp')).astype(jnp.bfloat16)]
    all_gather x0 -> x1, waiting for transfers between devices: none -> 16.8 us  [shards(): all_gather(partial_value, ('tp', 'grp'))]
    all_to_all x1, waiting for transfers between devices: 0.01 us -> 4.19 us  [shards(): lax.all_to_all(merged.reshape(ctx_size, bucket_rows, -1), 'ctx', split_ax...]
    all_gather x1, waiting for transfers between devices: 12.1 us -> 10.8 us  [shards(): text_full = lax.all_gather(text_states, ('tp', 'grp'), axis=1, tiled=True)]
    reduce_sum x0 -> x1, other arithmetic: none -> 1.28 us  [shards(): jnp.sum(all_gather(partial_value, ('tp', 'grp')), axis=0)]
  transfers between devices with their start and end apart: 2 -> 3, of which waited for: 1 -> 3; matrix products, arithmetic and copies ran while one was open for 10% -> 13% of each run, Pallas kernels for 0% -> 0%
where the time goes in v1:
time: 95.6 us; the launch traced here: 95.1 us
  waiting for transfers between devices  32.5 us (34%)
  matrix products  14.1 us (15%)
  between operations  13.7 us (14%)
  local copies, waits for them, and re-layouts  13 us (14%)
  blocking collectives  9.63 us (10%)
  other arithmetic  8.6 us (9%)
  starting transfers between devices  3.7 us (4%)
    all_gather x1, waiting for transfers between devices, shards(): all_gather(partial_value, ('tp', 'grp'))  16.8 us
    all_gather x1, waiting for transfers between devices, shards(): text_full = lax.all_gather(text_states, ('tp', 'grp'), axis=1, tiled=True)  10.8 us
    all_gather x1, blocking collectives, shards(): shard_piece = lax.all_gather(chosen, 'ctx', axis=0, tiled=True)  9.63 us
    dot_general x1, matrix products, shards(): jnp.dot(hidden, merge_down, preferred_element_type=jnp.float32)  4.57 us
    all_to_all x1, waiting for transfers between devices, shards(): lax.all_to_all(merged.reshape(ctx_size, bucket_rows, -1), 'ctx', split_ax...  4.19 us
    all_to_all x1, starting transfers between devices, shards(): lax.all_to_all(merged.reshape(ctx_size, bucket_rows, -1), 'ctx', split_ax...  3.66 us
    gather x1, local copies, waits for them, and re-layouts, attend(): key_seg = segment_ids[key_pos]  3.49 us
    dot_general x1, matrix products, shards(): jnp.dot(normal, kv_weight, preferred_element_type=jnp.float32)  3.35 us
  transfers between devices with their start and end apart: 3, of which 3 were waited for; matrix products, arithmetic and copies ran while one was open for 13% of the time, Pallas kernels for 0%

profile of v1, /device:TPU:0, one launch (start us, length us, event | category | flops | bytes accessed | tf_op | source)
XLA Modules:
  0.0 95.1 jit_solution(283522146798433267)
XLA Ops:
  6.5 1.0 %convert_multiply_fusion.3 = f32[8,5120]{1,0:T(8,128)S(1)} fusion(bf16[8,5120]{1,0:T(8,128)(2,1)} %param.10), kind=kLoop, calls=%fused_computation.30 | loop fusion | flops 81920 | bytes 245760 | tf_op jit(solution)/shard_map/mul | solution.py:15
  7.6 0.1 reduce_sum.76
  7.7 0.7 mul.112
  8.5 4.6 %fusion.41 = f32[8,4096]{1,0:T(8,128)} fusion(bf16[320,4096]{1,0:T(8,128)(2,1)} %param.16, bf16[5120,320]{0,1:T(8,128)(2,1)S(1)} %copy-done, f32[8,5120]{1,0:T(8,128)S(1)} %bitcast.61, bf16[8,5120]{1,0:T(8,128)(2,1)} %param.10, f32[5120]{0:T(1024)S(1)} %mul.113), kind=kOutput, calls=%fused_computation.59 | convolution fusion | flops 47516160 | bytes 6295552 | tf_op jit(solution)/shard_map/dot_general | solution.py:97
  13.2 0.7 all-gather.4.cloned.1.call-update
  13.9 0.2 fusion.112
  14.1 0.1 reduce.2
  14.2 0.6 slice.10
  14.9 1.3 %gather_fusion = s32[128]{0:T(128)S(1)} fusion(s32[512]{0:T(512)S(1)} %copy-done.1, s32[1024]{0:T(1024)S(1)} %pad_clamp_fusion.1), kind=kCustom, calls=%fused_computation | custom fusion | bytes 1536 | tf_op jit(solution)/shard_map/gather | solution.py:122
  16.2 3.5 %gather_fusion.1 = s32[512]{0:T(512)S(1)} fusion(s32[512]{0:T(512)S(1)} %copy-done.1, s32[1024]{0:T(1024)S(1)} %pad_clamp_fusion), kind=kCustom, calls=%fused_computation.1 | custom fusion | bytes 6144 | tf_op jit(solution)/shard_map/gather | solution.py:40
  19.8 0.1 select_reduce_fusion.1
  19.9 0.6 fusion.80
  20.6 0.8 fusion.19
  21.4 16.8 %all-gather.6.cloned.1.call-done = f32[64,4096]{1,0:T(8,128)} async-done(((f32[8,4096]{1,0:T(8,128)}), f32[64,4096]{1,0:T(8,128)}) %all-gather.6.cloned.1.call-update) | async-done | bytes 1048592 | tf_op jit(solution)/shard_map/all_gather | solution.py:108
  38.2 1.3 %bitcast_reduce_fusion = bf16[8,4096]{1,0:T(8,128)(2,1)S(1)} fusion(f32[64,4096]{1,0:T(8,128)} %all-gather.6.cloned.1.call-done), kind=kLoop, calls=%fused_computation.16 | loop fusion | flops 229376 | bytes 1114112 | tf_op jit(solution)/shard_map/reduce_sum | solution.py:108
  39.5 0.7 convert_element_type.44
  40.2 3.7 %all-to-all-start = ((bf16[4,2,4096]{2,1,0:T(2,128)(2,1)}), bf16[4,2,4096]{2,1,0:T(2,128)(2,1)S(1)}, u32[]{:S(2)}, u32[]{:S(2)}) async-start(bf16[4,2,4096]{2,1,0:T(2,128)(2,1)} %convert_element_type.44), calls=%async_computation | async-start | bytes 131072 | tf_op jit(solution)/shard_map/all_to_all | solution.py:109
  43.9 0.6 iota_compare_fusion.4
  44.5 4.2 %all-to-all-done = bf16[4,2,4096]{2,1,0:T(2,128)(2,1)S(1)} async-done(((bf16[4,2,4096]{2,1,0:T(2,128)(2,1)}), bf16[4,2,4096]{2,1,0:T(2,128)(2,1)S(1)}, u32[]{:S(2)}, u32[]{:S(2)}) %all-to-all-start) | async-done | bytes 65568 | tf_op jit(solution)/shard_map/all_to_all | solution.py:109
  48.8 2.2 %gather_fusion.2 = bf16[128,4096]{1,0:T(8,128)(2,1)} fusion(bf16[8,4096]{1,0:T(8,128)(2,1)S(1)} %reshape.183, s32[1024]{0:T(1024)S(1)} %pad_clamp_fusion.2), kind=kCustom, calls=%fused_computation.2 | custom fusion | bytes 2097664 | tf_op jit(solution)/shard_map/gather | solution.py:114
  51.0 10.8 %all-gather.4.cloned.1.call-done = bf16[128,4096]{1,0:T(8,128)(2,1)} async-done(((bf16[128,512]{1,0:T(8,128)(2,1)}), bf16[128,4096]{1,0:T(8,128)(2,1)}) %all-gather.4.cloned.1.call-update) | async-done | bytes 1048592 | tf_op jit(solution)/shard_map/all_gather | solution.py:113
  61.7 2.2 %fusion = (f32[128]{0:T(128)S(1)}, bf16[128,4096]{1,0:T(8,128)(2,1)S(1)}) fusion(bf16[128,4096]{1,0:T(8,128)(2,1)} %gather_fusion.2, bf16[128,4096]{1,0:T(8,128)(2,1)} %all-gather.4.cloned.1.call-done, pred[128]{0:T(512)(128)(4,1)S(1)} %iota_compare_fusion.4), kind=kLoop, calls=%fused_computation.5 | loop fusion | flops 2097024 | bytes 3146368 | tf_op jit(solution)/shard_map/reduce_sum | solution.py:15
  63.9 3.3 %fusion.16 = bf16[128,512]{1,0:T(8,128)(2,1)S(1)} fusion(bf16[4096,512]{1,0:T(8,128)(2,1)} %param.19, bf16[128,4096]{1,0:T(8,128)(2,1)S(1)} %get-tuple-element.6, f32[4096]{0:T(1024)S(1)} %copy-done.6, f32[128]{0:T(128)S(1)} %add_rsqrt_fusion.1), kind=kOutput, calls=%fused_computation.25 | convolution fusion | flops 538968064 | bytes 5390848 | tf_op jit(solution)/shard_map/dot_general | solution.py:117
  67.3 9.6 %all_gather.15 = bf16[512,256]{1,0:T(8,128)(2,1)} all-gather(bf16[128,256]{1,0:T(8,128)(2,1)S(1)} %dynamic-slice_convert_fusion), channel_id=1, replica_groups=mesh['ctx'=4,'tp'=4,'grp'=2] {'ctx'}, dimensions={0}, use_global_device_ids=true | all-gather | bytes 327680 | tf_op jit(solution)/shard_map/all_gather | solution.py:127
  77.0 1.0 %reshape.184 = bf16[512,1,2,128]{3,2,0,1:T(2,128)(2,1)S(1)} reshape(bf16[512,256]{1,0:T(8,128)(2,1)} %all_gather.15) | data formatting | bytes 524288 | tf_op jit(solution)/shard_map/reshape | solution.py:33
  78.0 1.1 %fusion.113 = (bf16[512,1,1,128]{3,2,0,1:T(2,128)(2,1)}, bf16[512,1,1,128]{3,2,0,1:T(2,128)(2,1)S(1)}) fusion(bf16[512,1,2,128]{3,2,0,1:T(2,128)(2,1)S(1)} %reshape.184), kind=kLoop, calls=%fused_computation.156 | loop fusion | bytes 524288 | tf_op jit(solution)/shard_map/slice | solution.py:35
  79.1 3.3 %fusion.7 = bf16[16,4,8,128]{3,2,1,0:T(8,128)(2,1)S(1)} fusion(bf16[4096,512]{1,0:T(8,128)(2,1)} %param.18, bf16[128,4096]{1,0:T(8,128)(2,1)} %copy-done.2, f32[4096]{0:T(1024)S(1)} %copy-done.6, f32[128]{0:T(128)} %copy-done.7), kind=kOutput, calls=%fused_computation.15 | convolution fusion | flops 539033600 | bytes 5390848 | tf_op jit(solution)/shard_map/dot_general | solution.py:116
  82.4 1.3 %fusion.114 = (f32[4,128]{1,0:T(4,128)S(1)}, f32[1,4,128,512]{2,3,1,0:T(8,128)}) fusion(bf16[16,4,8,128]{3,2,1,0:T(8,128)(2,1)S(1)} %fusion.7, bf16[512,1,1,128]{3,2,0,1:T(2,128)(2,1)S(1)} %get-tuple-element.10, pred[128,512]{0,1:T(8,128)(4,1)S(1)} %copy-done.4), kind=kOutput, calls=%fused_computation.157 | convolution fusion | flops 67894784 | bytes 1378304 | tf_op jit(solution)/shard_map/qkgd,rkd->kgqr/dot_general | solution.py:46
  83.7 0.8 copy.27
  84.5 1.4 %fusion.8 = f32[4,128]{1,0:T(4,128)S(1)} fusion(f32[1,4,128,512]{2,3,1,0:T(8,128)} %get-tuple-element.12, f32[4,128]{1,0:T(4,128)S(1)} %broadcast_maximum_fusion, pred[128,512]{0,1:T(8,128)(4,1)} %fusion.19), kind=kLoop, calls=%fused_computation.19 | loop fusion | flops 785920 | bytes 1118208 | tf_op jit(solution)/shard_map/reduce_sum | solution.py:52
  85.9 1.6 %fusion.6 = bf16[128,4,128]{0,2,1:T(8,128)(2,1)S(1)} fusion(f32[1,4,128,512]{2,3,1,0:T(8,128)} %get-tuple-element.12, f32[4,128]{1,0:T(4,128)S(1)} %broadcast_maximum_fusion, pred[128,512]{0,1:T(8,128)(4,1)} %fusion.19, bf16[512,1,1,128]{0,3,2,1:T(8,128)(2,1)} %copy.27, f32[128,4]{0,1:T(4,128)S(1)} %bitcast.64), kind=kOutput, calls=%fused_computation.13 | convolution fusion | flops 68026368 | bytes 1380352 | tf_op jit(solution)/shard_map/kgqr,rkd->kgqd/dot_general | solution.py:53
  87.5 0.8 copy.25
  (40 shorter events, 0.5 us)
Async XLA Ops:
  6.5 2.0 %copy-start = (bf16[5120,320]{0,1:T(8,128)(2,1)S(1)}, bf16[5120,320]{0,1:T(8,128)(2,1)}, u32[]{:S(2)}) copy-start(bf16[5120,320]{0,1:T(8,128)(2,1)} %param.15) | copy-start | bytes 9830404
  6.5 31.7 %all-gather.6.cloned.1.call-start = ((), (), s32[]{:S(2)}) async-start(), calls=%async_computation.2 | async-start | bytes 1179648 | tf_op jit(solution)/shard_map/all_gather | solution.py:108
  8.5 5.4 %copy-start.5 = (s32[4,4]{1,0:T(4,128)S(1)}, s32[4,4]{1,0:T(4,128)}, u32[]{:S(2)}) copy-start(s32[4,4]{1,0:T(4,128)} %param.11) | copy-start | bytes 196
  8.5 6.4 %copy-start.1 = (s32[512]{0:T(512)S(1)}, s32[512]{0:T(512)}, u32[]{:S(2)}) copy-start(s32[512]{0:T(512)} %param.13) | copy-start | bytes 6148
  13.1 48.6 %all-gather.4.cloned.1.call-start = ((), (), s32[]{:S(2)}) async-start(), calls=%async_computation.1 | async-start | bytes 1179648 | tf_op jit(solution)/shard_map/all_gather | solution.py:113
  40.2 8.5 %all-to-all-start = ((bf16[4,2,4096]{2,1,0:T(2,128)(2,1)}), bf16[4,2,4096]{2,1,0:T(2,128)(2,1)S(1)}, u32[]{:S(2)}, u32[]{:S(2)}) async-start(bf16[4,2,4096]{2,1,0:T(2,128)(2,1)} %convert_element_type.44), calls=%async_computation | async-start | bytes 131072 | tf_op jit(solution)/shard_map/all_to_all | solution.py:109
  51.0 13.0 %copy-start.6 = (f32[4096]{0:T(1024)S(1)}, f32[4096]{0:T(1024)}, u32[]{:S(2)}) copy-start(f32[4096]{0:T(1024)} %param.17) | copy-start | bytes 49156
  63.9 3.4 %copy-start.2 = (bf16[128,4096]{1,0:T(8,128)(2,1)}, bf16[128,4096]{1,0:T(8,128)(2,1)S(1)}, u32[]{:S(2)}) copy-start(bf16[128,4096]{1,0:T(8,128)(2,1)S(1)} %get-tuple-element.6) | copy-start | bytes 3145732
  63.9 3.4 %copy-start.7 = (f32[128]{0:T(128)}, f32[128]{0:T(128)S(1)}, u32[]{:S(2)}) copy-start(f32[128]{0:T(128)S(1)} %add_rsqrt_fusion.1) | copy-start | bytes 1540
  79.1 3.3 %copy-start.4 = (pred[128,512]{0,1:T(8,128)(4,1)S(1)}, pred[128,512]{0,1:T(8,128)(4,1)}, u32[]{:S(2)}) copy-start(pred[128,512]{0,1:T(8,128)(4,1)} %fusion.19) | copy-start | bytes 196612
  79.1 4.6 %copy-start.3 = (bf16[512,1,1,128]{3,2,0,1:T(2,128)(2,1)S(1)}, bf16[512,1,1,128]{3,2,0,1:T(2,128)(2,1)}, u32[]{:S(2)}) copy-start(bf16[512,1,1,128]{3,2,0,1:T(2,128)(2,1)} %get-tuple-element.9) | copy-start | bytes 393220
Sparse Core Ops, SparseCore 0:
  13.3 24.9 all-gather.5
  39.9 21.8 all-gather.3
